TPU v7x, 32 devices: a whole 2x2x4 slice. The times are simulated.
32 devices in a mesh: cuts: 2 (over x), frame: 8 (over z, y), coil: 2 (over core).
Axes of the slice: x: 2, y: 2, z: 4, core: 2. Of those that a mesh axis runs over, the one named last changes fastest.
Arguments:
- spatial: bfloat16 [512, 32, 512], P(('cuts', 'coil', 'frame')), parts along dimension 0, may hold values from -6 to 6
- temporal: bfloat16 [32, 64], P(('cuts', 'frame')), parts along dimension 0, may hold values from -0.75 to 0.75
- kspace: bfloat16 [32, 32, 256, 512], P(('cuts', 'frame'), 'coil'), parts along dimension 0, may hold values from -2 to 2
- sampled: int32 [32, 256], P(('cuts', 'frame')), parts along dimension 0, may hold values 0 or 1
- sensitivity: bfloat16 [64, 256, 512], P(('cuts', 'coil')), parts along dimension 0, may hold values from -1 to 1
Outputs:
- spatial_grad: float32 [512, 32, 512], P(('cuts', 'coil', 'frame')), parts along dimension 0
- temporal_grad: float32 [32, 64], P(('cuts', 'frame')), parts along dimension 0
There are 2 independent parts, one for each index of `cuts`. A program takes and returns all parts, laid end to end along the dimension named above; each array names one. Nothing has to cross between parts.
All inputs are finite; a program needn't handle non-finite values. No bound on the sum of `sampled` on one device may be relied on, other than what follows from the above.
Results may differ from a plain program's by a relative error of at most 0.003.
Values may be sent and summed in bfloat16 or wider, within the bound.
No kernel may reach another device: no remote copies, remote signals or barrier semaphores. Data moves between devices by JAX's collectives and lax.ppermute only.
A program may use at most 128 MiB of HBM per device.

v0:
```python
import math
import jax
import jax.numpy as jnp
from jax import lax
from jax.sharding import PartitionSpec as P


def split_parts(values):
    half_width = values.shape[-1] // 2
    return (values[..., :half_width], values[..., half_width:])


def dft_block(length):
    index = jnp.arange(length, dtype=jnp.int32)
    angles = (index[:, None] * index[None, :] % length).astype(jnp.float32) * (
        2.0 * math.pi / length
    )
    norm_factor = 1.0 / math.sqrt(length)
    cosine = jnp.cos(angles) * norm_factor
    sine_part = -jnp.sin(angles) * norm_factor
    upper_rows = jnp.concatenate([cosine, sine_part], 1)
    lower_rows = jnp.concatenate([-sine_part, cosine], 1)
    return jnp.concatenate([upper_rows, lower_rows], 0).astype(jnp.bfloat16)


def to_image(temporal, spatial):
    temp_real, temp_imag = split_parts(temporal)
    spat_real, spat_imag = split_parts(spatial)
    image_real = jnp.einsum(
        "tr,xry->txy", temp_real, spat_real, preferred_element_type=jnp.float32
    ) - jnp.einsum("tr,xry->txy", temp_imag, spat_imag, preferred_element_type=jnp.float32)
    image_imag = jnp.einsum(
        "tr,xry->txy", temp_real, spat_imag, preferred_element_type=jnp.float32
    ) + jnp.einsum("tr,xry->txy", temp_imag, spat_real, preferred_element_type=jnp.float32)
    return jnp.concatenate([image_real, image_imag], -1).astype(jnp.bfloat16)


def factor_grad(temporal, grad_image):
    temp_real, temp_imag = split_parts(temporal)
    grad_real, grad_imag = split_parts(grad_image)
    spatial_real = jnp.einsum(
        "tr,txy->xry", temp_real, grad_real, preferred_element_type=jnp.float32
    ) + jnp.einsum("tr,txy->xry", temp_imag, grad_imag, preferred_element_type=jnp.float32)
    spatial_imag = jnp.einsum(
        "tr,txy->xry", temp_real, grad_imag, preferred_element_type=jnp.float32
    ) - jnp.einsum("tr,txy->xry", temp_imag, grad_real, preferred_element_type=jnp.float32)
    return jnp.concatenate([spatial_real, spatial_imag], -1)


def frame_grad(spatial, grad_image):
    spat_real, spat_imag = split_parts(spatial)
    grad_real, grad_imag = split_parts(grad_image)
    temporal_real = jnp.einsum(
        "xry,txy->tr", spat_real, grad_real, preferred_element_type=jnp.float32
    ) + jnp.einsum("xry,txy->tr", spat_imag, grad_imag, preferred_element_type=jnp.float32)
    temporal_imag = jnp.einsum(
        "xry,txy->tr", spat_real, grad_imag, preferred_element_type=jnp.float32
    ) - jnp.einsum("xry,txy->tr", spat_imag, grad_real, preferred_element_type=jnp.float32)
    return jnp.concatenate([temporal_real, temporal_imag], -1)


def coil_adjoint(image, measured, sampled_row, sensitivity, block):
    image_real, image_imag = split_parts(image.astype(jnp.float32))
    sens_real, sens_imag = split_parts(sensitivity.astype(jnp.float32))
    coil_real = sens_real * image_real[None] - sens_imag * image_imag[None]
    coil_imag = sens_real * image_imag[None] + sens_imag * image_real[None]
    coil_image = jnp.concatenate([coil_real, coil_imag], -1).astype(jnp.bfloat16)
    coil_count, row_count, full_width = coil_image.shape
    spectrum = jnp.dot(
        coil_image.reshape(coil_count * row_count, full_width),
        block,
        preferred_element_type=jnp.float32,
    ).reshape(coil_count, row_count, full_width)
    line_keep = jnp.concatenate([sampled_row, sampled_row]).astype(jnp.float32)
    misfit = (line_keep * (spectrum - measured.astype(jnp.float32))).astype(jnp.bfloat16)
    adjoint = jnp.dot(
        misfit.reshape(coil_count * row_count, full_width),
        block.T,
        preferred_element_type=jnp.float32,
    ).reshape(coil_count, row_count, full_width)
    back_real, back_imag = split_parts(adjoint)
    grad_real = jnp.sum(sens_real * back_real + sens_imag * back_imag, axis=0)
    grad_imag = jnp.sum(sens_real * back_imag - sens_imag * back_real, axis=0)
    return jnp.concatenate([grad_real, grad_imag], -1)


def on_device(spatial, temporal, kspace, sampled, sensitivity):
    block = dft_block(spatial.shape[2] // 2)
    temporal_all = lax.all_gather(temporal, "frame", axis=0, tiled=True)
    image_rows = to_image(temporal_all, spatial)
    image_half = lax.all_to_all(image_rows, "frame", split_axis=0, concat_axis=1, tiled=True)
    image_full = lax.all_gather(image_half, "coil", axis=1, tiled=True)
    coil_partial = lax.map(
        lambda frame_item: coil_adjoint(
            frame_item[0], frame_item[1], frame_item[2], sensitivity, block
        ),
        (image_full, kspace, sampled),
    )
    grad_half = lax.psum_scatter(coil_partial, "coil", scatter_dimension=1, tiled=True).astype(
        jnp.bfloat16
    )
    grad_rows = lax.all_to_all(grad_half, "frame", split_axis=1, concat_axis=0, tiled=True)
    spatial_grad = factor_grad(temporal_all, grad_rows)
    temporal_part = lax.psum_scatter(
        frame_grad(spatial, grad_rows), "frame", scatter_dimension=0, tiled=True
    )
    temporal_grad = lax.psum(temporal_part, "coil")
    return (spatial_grad, temporal_grad)


def solution(mesh):
    placed = (
        P(("cuts", "coil", "frame"), None, None),
        P(("cuts", "frame"), None),
        P(("cuts", "frame"), "coil", None, None),
        P(("cuts", "frame"), None),
        P(("cuts", "coil"), None, None),
    )
    return jax.shard_map(
        on_device,
        mesh=mesh,
        in_specs=placed,
        out_specs=(P(("cuts", "coil", "frame"), None, None), P(("cuts", "frame"), None)),
        check_vma=False,
    )
```

profile of v0, /device:TPU:0, one launch (start us, length us, event | category | flops | bytes accessed | tf_op | source)
XLA Modules:
  0.0 152.4 jit_solution(3036720703098302424)
XLA Ops:
  0.6 22.5 %all-gather = bf16[8,2,64]{2,1,0:T(2,128)(2,1)S(1)} all-gather(bf16[1,2,64]{2,1,0:T(2,128)(2,1)} %bitcast.83), channel_id=1, replica_groups=mesh['cuts'=2,'frame'=8,'coil'=2] {'frame'}, dimensions={0}, use_global_device_ids=true | all-gather | bytes 2304 | tf_op jit(solution)/shard_map/all_gather | solution.py:89
  23.1 1.1 fusion.41
  24.2 1.1 fusion.35
  25.3 1.2 fusion.22
  26.5 1.2 fusion.23
  28.6 3.4 %all-to-all-start = ((bf16[16,16,512]{2,1,0:T(8,128)(2,1)}), bf16[16,16,512]{2,1,0:T(8,128)(2,1)S(1)}, u32[]{:S(2)}, u32[]{:S(2)}) async-start(bf16[16,16,512]{2,1,0:T(8,128)(2,1)} %copy.13), calls=%async_computation | async-start | bytes 524288 | tf_op jit(solution)/shard_map/all_to_all | solution.py:91
  32.0 1.3 dynamic-slice
  33.9 1.0 fusion.32
  34.9 1.1 negate_convert_fusion
  36.9 3.3 %all-to-all-done = bf16[16,16,512]{2,1,0:T(8,128)(2,1)S(1)} async-done(((bf16[16,16,512]{2,1,0:T(8,128)(2,1)}), bf16[16,16,512]{2,1,0:T(8,128)(2,1)S(1)}, u32[]{:S(2)}, u32[]{:S(2)}) %all-to-all-start) | async-done | bytes 262176 | tf_op jit(solution)/shard_map/all_to_all | solution.py:91
  40.2 2.2 %all_gather.7 = bf16[2,256,512]{2,1,0:T(8,128)(2,1)S(1)} all-gather(bf16[2,128,512]{2,1,0:T(8,128)(2,1)S(1)} %bitcast.70), channel_id=1, replica_groups=mesh['cuts'=2,'frame'=8,'coil'=2] {'coil'}, dimensions={1}, use_global_device_ids=true | all-gather | bytes 786432 | tf_op jit(solution)/shard_map/all_gather | solution.py:92
  42.4 62.9 %while.10 = (s32[]{:T(128)}, f32[2,256,512]{2,0,1:T(2,128)}, bf16[16,256,512]{2,1,0:T(8,128)(2,1)}, s32[2,256]{1,0:T(2,128)S(1)}, bf16[2,256,512]{2,1,0:T(8,128)...) while((s32[]{:T(128)}, f32[2,256,512]{2,0,1:T(2,128)}, ...), condition=%wide.region_3.4_spmd, body=%wide.region_0.3_spmd.sunk | while | flops 4330750976 | bytes 107749048 | solution.py:93
  42.5 3.4 %convert_element_type.64 = f32[16,256,512]{2,1,0:T(8,128)S(1)} convert(bf16[16,256,512]{2,1,0:T(8,128)(2,1)} %get-tuple-element.137) | non-fusion elementwise | flops 2097152 | bytes 12582912 | tf_op jit(solution)/shard_map/while/body/eval_jaxpr/convert_element_type | solution.py:64
  45.9 3.0 %subtract_convert_fusion.2 = (bf16[16,256,256]{2,1,0:T(8,128)(2,1)S(1)}, bf16[16,256,256]{2,1,0:T(8,128)(2,1)}) fusion(f32[16,256,512]{2,1,0:T(8,128)S(1)} %convert_element_type.64, f32[256,256]{1,0:T(8,128)S(1)} %get-tuple-element.111, f32[256,256]{1,0:T(8,128)S(1)} %get-tuple-element.112), kind=kLoop, calls=%fused_computation.13.clone.1 | loop fusion | flops 8388608 | bytes 13107200 | tf_op jit(solution)/shard_map/convert.2
  48.8 0.9 copy-done
  49.7 10.8 %fusion.65 = f32[16,256,512]{2,1,0:T(8,128)} fusion(bf16[2,16,256,512]{3,2,1,0:T(8,128)(2,1)} %get-tuple-element.141, s32[]{:T(128)} %get-tuple-element.126, f32[512]{0:T(512)S(1)} %add_convert_fusion.3, bf16[16,256,256]{2,1,0:T(8,128)(2,1)} %get-tuple-element.113, bf16[16,256,256]{2,1,0:T(8,128)(2,1)S(1)} %get-tuple-element.114, ...), kind=kOutput, calls=%fused_computation.3.clone.1 | convolution fusion | flops 4311744512 | bytes 17828352 | tf_op jit(solution)/shard_map/while/body/eval_jaxpr/dot_general | solution.py:76
  60.5 7.0 %add_reduce_fusion.2 = (f32[256,256]{1,0:T(8,128)S(1)}, f32[256,256]{1,0:T(8,128)S(1)}) fusion(f32[16,256,512]{2,1,0:T(8,128)} %fusion.65, f32[16,256,512]{2,1,0:T(8,128)} %copy-done), kind=kLoop, calls=%fused_computation.10.clone.1 | loop fusion | flops 8257536 | bytes 17301504 | tf_op jit(solution)/shard_map/while/body/eval_jaxpr/reduce_sum | solution.py:82
  68.2 4.7 %dynamic_update_slice.5 = f32[2,256,512]{2,0,1:T(2,128)S(1)} dynamic-update-slice(f32[2,256,512]{2,0,1:T(2,128)S(1)} %copy-done.2, f32[1,256,512]{2,0,1:T(1,128)S(1)} %copy.22, s32[]{:T(128)} %get-tuple-element.126, s32[]{:T(128)} %constant.31.clone.1..sunk, s32[]{:T(128)} %constant.31.clone.1..sunk) | dynamic-update-slice | bytes 1048580 | tf_op jit(solution)/shard_map/while/body/jit(dynamic_update_index_in_dim)/dynamic_update_slice | solution.py:93
  72.9 1.0 copy-done.3
  74.0 3.3 %convert_element_type.64 = f32[16,256,512]{2,1,0:T(8,128)S(1)} convert(bf16[16,256,512]{2,1,0:T(8,128)(2,1)} %get-tuple-element.137) | non-fusion elementwise | flops 2097152 | bytes 12582912 | tf_op jit(solution)/shard_map/while/body/eval_jaxpr/convert_element_type | solution.py:64
  77.3 3.0 %subtract_convert_fusion.2 = (bf16[16,256,256]{2,1,0:T(8,128)(2,1)S(1)}, bf16[16,256,256]{2,1,0:T(8,128)(2,1)}) fusion(f32[16,256,512]{2,1,0:T(8,128)S(1)} %convert_element_type.64, f32[256,256]{1,0:T(8,128)S(1)} %get-tuple-element.111, f32[256,256]{1,0:T(8,128)S(1)} %get-tuple-element.112), kind=kLoop, calls=%fused_computation.13.clone.1 | loop fusion | flops 8388608 | bytes 13107200 | tf_op jit(solution)/shard_map/convert.2
  81.2 10.8 %fusion.65 = f32[16,256,512]{2,1,0:T(8,128)} fusion(bf16[2,16,256,512]{3,2,1,0:T(8,128)(2,1)} %get-tuple-element.141, s32[]{:T(128)} %get-tuple-element.126, f32[512]{0:T(512)S(1)} %add_convert_fusion.3, bf16[16,256,256]{2,1,0:T(8,128)(2,1)} %get-tuple-element.113, bf16[16,256,256]{2,1,0:T(8,128)(2,1)S(1)} %get-tuple-element.114, ...), kind=kOutput, calls=%fused_computation.3.clone.1 | convolution fusion | flops 4311744512 | bytes 17828352 | tf_op jit(solution)/shard_map/while/body/eval_jaxpr/dot_general | solution.py:76
  91.9 7.0 %add_reduce_fusion.2 = (f32[256,256]{1,0:T(8,128)S(1)}, f32[256,256]{1,0:T(8,128)S(1)}) fusion(f32[16,256,512]{2,1,0:T(8,128)} %fusion.65, f32[16,256,512]{2,1,0:T(8,128)} %copy-done), kind=kLoop, calls=%fused_computation.10.clone.1 | loop fusion | flops 8257536 | bytes 17301504 | tf_op jit(solution)/shard_map/while/body/eval_jaxpr/reduce_sum | solution.py:82
  99.6 4.7 %dynamic_update_slice.5 = f32[2,256,512]{2,0,1:T(2,128)S(1)} dynamic-update-slice(f32[2,256,512]{2,0,1:T(2,128)S(1)} %copy-done.2, f32[1,256,512]{2,0,1:T(1,128)S(1)} %copy.22, s32[]{:T(128)} %get-tuple-element.126, s32[]{:T(128)} %constant.31.clone.1..sunk, s32[]{:T(128)} %constant.31.clone.1..sunk) | dynamic-update-slice | bytes 1048580 | tf_op jit(solution)/shard_map/while/body/jit(dynamic_update_index_in_dim)/dynamic_update_slice | solution.py:93
  104.3 1.0 copy-done.3
  105.3 6.9 %all-reduce.3 = bf16[2,256,512]{2,0,1:T(2,128)(2,1)S(1)} all-reduce(f32[2,256,512]{2,0,1:T(2,128)} %get-tuple-element.39), channel_id=2, replica_groups=mesh['cuts'=2,'frame'=8,'coil'=2] {'coil'}, use_global_device_ids=true, to_apply=%region_4.5.clone | all-reduce | flops 262144 | bytes 1572864
  112.2 0.9 dynamic-slice_convert_fusion
  113.1 3.4 %all-to-all-start.1 = ((bf16[2,128,512]{2,0,1:T(2,128)(2,1)}), bf16[2,128,512]{2,0,1:T(2,128)(2,1)S(1)}, u32[]{:S(2)}, u32[]{:S(2)}) async-start(bf16[2,128,512]{2,0,1:T(2,128)(2,1)} %dynamic-slice_convert_fusion), calls=%async_computation.1 | async-start | bytes 524288 | tf_op jit(solution)/shard_map/all_to_all | solution.py:102
  117.7 8.4 %all-to-all-done.1 = bf16[2,128,512]{2,0,1:T(2,128)(2,1)S(1)} async-done(((bf16[2,128,512]{2,0,1:T(2,128)(2,1)}), bf16[2,128,512]{2,0,1:T(2,128)(2,1)S(1)}, u32[]{:S(2)}, u32[]{:S(2)}) %all-to-all-start.1) | async-done | bytes 262176 | tf_op jit(solution)/shard_map/all_to_all | solution.py:102
  127.9 19.6 %all-reduce.1 = f32[16,64]{1,0:T(8,128)S(1)} all-reduce(f32[16,64]{1,0:T(8,128)S(1)} %pad_maximum_fusion.2), channel_id=3, replica_groups=mesh['cuts'=2,'frame'=8,'coil'=2] {'frame'}, use_global_device_ids=true, to_apply=%region_5.6.clone | all-reduce | flops 1024 | bytes 8192
  147.6 3.0 %psum.7 = f32[2,64]{1,0:T(2,128)} all-reduce(f32[2,64]{1,0:T(2,128)S(1)} %constant_dynamic-slice_fusion.1), channel_id=1, replica_groups=mesh['cuts'=2,'frame'=8,'coil'=2] {'coil'}, use_global_device_ids=true, to_apply=%region_6.7 | all-reduce | flops 128 | bytes 1024 | tf_op jit(solution)/shard_map/psum | solution.py:107
  151.3 1.1 pad_maximum_fusion
  (45 shorter events, 7.0 us)
Async XLA Ops:
  0.6 41.7 %copy-start.4 = (s32[2,256]{1,0:T(2,128)S(1)}, s32[2,256]{1,0:T(2,128)}, u32[]{:S(2)}) copy-start(s32[2,256]{1,0:T(2,128)} %param.10) | copy-start | bytes 6148
  28.6 11.6 %all-to-all-start = ((bf16[16,16,512]{2,1,0:T(8,128)(2,1)}), bf16[16,16,512]{2,1,0:T(8,128)(2,1)S(1)}, u32[]{:S(2)}, u32[]{:S(2)}) async-start(bf16[16,16,512]{2,1,0:T(8,128)(2,1)} %copy.13), calls=%async_computation | async-start | bytes 524288 | tf_op jit(solution)/shard_map/all_to_all | solution.py:91
  42.4 74.1 %copy-start.5 = (u32[32]{0:T(128)S(1)}, u32[32]{0:T(128)}, u32[]{:S(2)}) copy-start(u32[32]{0:T(128)} %constant.47) | copy-start | bytes 388
  42.4 84.1 %copy-start.1 = (bf16[16,32,512]{2,1,0:T(8,128)(2,1)S(1)}, bf16[16,32,512]{2,1,0:T(8,128)(2,1)}, u32[]{:S(2)}) copy-start(bf16[16,32,512]{2,1,0:T(8,128)(2,1)} %param.7) | copy-start | bytes 1572868
  45.9 3.8 %copy-start = (f32[16,256,512]{2,1,0:T(8,128)}, f32[16,256,512]{2,1,0:T(8,128)S(1)}, u32[]{:S(2)}) copy-start(f32[16,256,512]{2,1,0:T(8,128)S(1)} %convert_element_type.64) | copy-start | bytes 25165828 | tf_op jit(solution)/shard_map/while
  60.5 7.6 %copy-start.2 = (f32[2,256,512]{2,0,1:T(2,128)S(1)}, f32[2,256,512]{2,0,1:T(2,128)}, u32[]{:S(2)}) copy-start(f32[2,256,512]{2,0,1:T(2,128)} %get-tuple-element.127) | copy-start | bytes 3145732 | tf_op jit(solution)/shard_map/while
  72.9 1.0 copy-start.3
  77.3 3.8 %copy-start = (f32[16,256,512]{2,1,0:T(8,128)}, f32[16,256,512]{2,1,0:T(8,128)S(1)}, u32[]{:S(2)}) copy-start(f32[16,256,512]{2,1,0:T(8,128)S(1)} %convert_element_type.64) | copy-start | bytes 25165828 | tf_op jit(solution)/shard_map/while
  91.9 7.6 %copy-start.2 = (f32[2,256,512]{2,0,1:T(2,128)S(1)}, f32[2,256,512]{2,0,1:T(2,128)}, u32[]{:S(2)}) copy-start(f32[2,256,512]{2,0,1:T(2,128)} %get-tuple-element.127) | copy-start | bytes 3145732 | tf_op jit(solution)/shard_map/while
  104.3 1.0 copy-start.3
  113.1 13.1 %all-to-all-start.1 = ((bf16[2,128,512]{2,0,1:T(2,128)(2,1)}), bf16[2,128,512]{2,0,1:T(2,128)(2,1)S(1)}, u32[]{:S(2)}, u32[]{:S(2)}) async-start(bf16[2,128,512]{2,0,1:T(2,128)(2,1)} %dynamic-slice_convert_fusion), calls=%async_computation.1 | async-start | bytes 524288 | tf_op jit(solution)/shard_map/all_to_all | solution.py:102
where the time goes:
time: 153 us; the launch traced here: 152 us
  blocking collectives  54.2 us (35%)
  other arithmetic  31 us (20%)
  matrix products  28.1 us (18%)
  local copies, waits for them, and re-layouts  18.2 us (12%)
  waiting for transfers between devices  11.7 us (8%)
  starting transfers between devices  6.82 us (4%)
  between operations  2.1 us (1%)
    unnamed x2, blocking collectives  26.5 us
    all_gather x1, blocking collectives, on_device(): temporal_all = lax.all_gather(temporal, 'frame', axis=0, tiled=True)  22.5 us
    dot_general x2, matrix products, coil_adjoint(): jnp.dot(misfit.reshape(coil_count * row_count, full_width), block.T, pref...  21.6 us
    reduce_sum x2, other arithmetic, coil_adjoint(): grad_real = jnp.sum(sens_real * back_real + sens_imag * back_imag, axis=0)  14 us
    dynamic_update_slice x4, local copies, waits for them, and re-layouts, on_device(): lax.map(lambda frame_item: coil_adjoint(frame_item[0], frame_item[1], fra...  10.5 us
    all_to_all x1, waiting for transfers between devices, on_device(): lax.all_to_all(grad_half, 'frame', split_axis=1, concat_axis=0, tiled=True)  8.41 us
    another operation x4, other arithmetic  8 us
    convert_element_type x2, other arithmetic, coil_adjoint(): sens_real, sens_imag = split_parts(sensitivity.astype(jnp.float32))  6.72 us
  transfers between devices with their start and end apart: 2, of which 2 were waited for; matrix products, arithmetic and copies ran while one was open for 3% of the time, Pallas kernels for 0%

commit v1 on v0

--- a/solution.py
+++ b/solution.py
@@ -1,8 +1,22 @@
+import functools
 import math
 import jax
 import jax.numpy as jnp
 from jax import lax
 from jax.sharding import PartitionSpec as P
+
+
+def lay_shards_for(packet, chip_axis):
+    local_part = jnp.concatenate(
+        lax.all_to_all(
+            jnp.stack(jnp.split(packet, lax.axis_size(chip_axis), 1), axis=0), chip_axis, 0, 0
+        ),
+        axis=0,
+    )
+    return local_part
+
+
+_plan_vector = functools.partial(lay_shards_for, chip_axis="frame")
 
 
 def split_parts(values):
@@ -99,7 +113,7 @@
     grad_half = lax.psum_scatter(coil_partial, "coil", scatter_dimension=1, tiled=True).astype(
         jnp.bfloat16
     )
-    grad_rows = lax.all_to_all(grad_half, "frame", split_axis=1, concat_axis=0, tiled=True)
+    grad_rows = _plan_vector(grad_half)
     spatial_grad = factor_grad(temporal_all, grad_rows)
     temporal_part = lax.psum_scatter(
         frame_grad(spatial, grad_rows), "frame", scatter_dimension=0, tiled=True

time: 153 us -> 163 us (1.065)
  between operations: 2.1 us -> 14.8 us
  waiting for transfers between devices: 11.7 us -> 20 us
  local copies, waits for them, and re-layouts: 18.2 us -> 10.2 us
  blocking collectives: 54.2 us -> 47.3 us
  starting transfers between devices: 6.82 us -> 9.29 us
    dynamic_update_slice x4 -> x0, local copies, waits for them, and re-layouts: 10.5 us -> none  [on_device(): lax.map(lambda frame_item: coil_adjoint(frame_item[0], frame_item[1], fra...]
    unnamed x2 -> x1, blocking collectives: 26.5 us -> 19.7 us
    reduce_scatter x0 -> x1, waiting for transfers between devices: none -> 6.79 us  [on_device(): lax.psum_scatter(coil_partial, 'coil', scatter_dimension=1, tiled=True)]
    unnamed x9 -> x15, local copies, waits for them, and re-layouts: 1.88 us -> 4.93 us
    all_to_all x1, starting transfers between devices: 3.41 us -> 5.84 us  [lay_shards_for(): lax.all_to_all(jnp.stack(jnp.split(packet, lax.axis_size(chip_axis), 1),...]
    all_to_all x1, waiting for transfers between devices: 3.29 us -> 5.16 us  [on_device(): lax.all_to_all(image_rows, 'frame', split_axis=0, concat_axis=1, tiled=True)]
  transfers between devices with their start and end apart: 2 -> 3, of which waited for: 2 -> 3; matrix products, arithmetic and copies ran while one was open for 3% -> 2% of each run, Pallas kernels for 0% -> 0%
where the time goes in v1:
time: 163 us; the launch traced here: 162 us
  blocking collectives  47.3 us (29%)
  other arithmetic  32.1 us (20%)
  matrix products  28.2 us (17%)
  waiting for transfers between devices  20 us (12%)
  between operations  14.8 us (9%)
  local copies, waits for them, and re-layouts  10.2 us (6%)
  starting transfers between devices  9.29 us (6%)
    all_gather x1, blocking collectives, on_device(): temporal_all = lax.all_gather(temporal, 'frame', axis=0, tiled=True)  22.5 us
    dot_general x2, matrix products, coil_adjoint(): jnp.dot(misfit.reshape(coil_count * row_count, full_width), block.T, pref...  21.6 us
    unnamed x1, blocking collectives  19.7 us
    reduce_sum x2, other arithmetic, coil_adjoint(): grad_real = jnp.sum(sens_real * back_real + sens_imag * back_imag, axis=0)  14 us
    all_to_all x1, waiting for transfers between devices, lay_shards_for(): lax.all_to_all(jnp.stack(jnp.split(packet, lax.axis_size(chip_axis), 1),...  8.08 us
    another operation x4, other arithmetic  7.96 us
    reduce_scatter x1, waiting for transfers between devices, on_device(): lax.psum_scatter(coil_partial, 'coil', scatter_dimension=1, tiled=True)  6.79 us
    convert_element_type x2, other arithmetic, coil_adjoint(): sens_real, sens_imag = split_parts(sensitivity.astype(jnp.float32))  6.72 us
  transfers between devices with their start and end apart: 3, of which 3 were waited for; matrix products, arithmetic and copies ran while one was open for 2% of the time, Pallas kernels for 0%

profile of v1, /device:TPU:0, one launch (start us, length us, event | category | flops | bytes accessed | tf_op | source)
XLA Modules:
  0.0 162.1 jit_solution(7080085500894493702)
XLA Ops:
  7.2 22.5 %all-gather = bf16[8,2,64]{2,1,0:T(2,128)(2,1)S(1)} all-gather(bf16[1,2,64]{2,1,0:T(2,128)(2,1)} %bitcast.110), channel_id=1, replica_groups=mesh['cuts'=2,'frame'=8,'coil'=2] {'frame'}, dimensions={0}, use_global_device_ids=true | all-gather | bytes 2304 | tf_op jit(solution)/shard_map/all_gather | solution.py:103
  29.6 1.1 fusion.42
  30.8 1.1 fusion.36
  31.9 1.2 fusion.23
  33.1 1.2 fusion.24
  34.3 0.8 copy.9
  35.1 3.4 %all-to-all-start = ((bf16[16,16,512]{2,1,0:T(8,128)(2,1)}), bf16[16,16,512]{2,1,0:T(8,128)(2,1)S(1)}, u32[]{:S(2)}, u32[]{:S(2)}) async-start(bf16[16,16,512]{2,1,0:T(8,128)(2,1)} %copy.9), calls=%async_computation | async-start | bytes 524288 | tf_op jit(solution)/shard_map/all_to_all | solution.py:105
  38.6 1.0 fusion.33
  39.6 1.1 negate_convert_fusion
  40.7 0.8 maximum_maximum_fusion
  41.5 5.2 %all-to-all-done = bf16[16,16,512]{2,1,0:T(8,128)(2,1)S(1)} async-done(((bf16[16,16,512]{2,1,0:T(8,128)(2,1)}), bf16[16,16,512]{2,1,0:T(8,128)(2,1)S(1)}, u32[]{:S(2)}, u32[]{:S(2)}) %all-to-all-start) | async-done | bytes 262176 | tf_op jit(solution)/shard_map/all_to_all | solution.py:105
  46.7 2.2 %all_gather.7 = bf16[2,256,512]{2,1,0:T(8,128)(2,1)S(1)} all-gather(bf16[2,128,512]{2,1,0:T(8,128)(2,1)S(1)} %bitcast.98), channel_id=1, replica_groups=mesh['cuts'=2,'frame'=8,'coil'=2] {'coil'}, dimensions={1}, use_global_device_ids=true | all-gather | bytes 786432 | tf_op jit(solution)/shard_map/all_gather | solution.py:106
  48.9 52.4 %while.10 = (s32[]{:T(128)}, f32[2,256,512]{2,1,0:T(8,128)}, bf16[16,256,512]{2,1,0:T(8,128)(2,1)}, s32[2,256]{1,0:T(2,128)S(1)}, bf16[2,256,512]{2,1,0:T(8,128)...) while((s32[]{:T(128)}, f32[2,256,512]{2,1,0:T(8,128)}, ...), condition=%wide.region_3.4_spmd, body=%wide.region_0.3_spmd.sunk | while | flops 4330750976 | bytes 105651888 | solution.py:107
  49.0 3.4 %convert_element_type.63 = f32[16,256,512]{2,1,0:T(8,128)S(1)} convert(bf16[16,256,512]{2,1,0:T(8,128)(2,1)} %get-tuple-element.137) | non-fusion elementwise | flops 2097152 | bytes 12582912 | tf_op jit(solution)/shard_map/while/body/eval_jaxpr/convert_element_type | solution.py:78
  52.4 2.9 %subtract_convert_fusion.2 = (bf16[16,256,256]{2,1,0:T(8,128)(2,1)S(1)}, bf16[16,256,256]{2,1,0:T(8,128)(2,1)}) fusion(f32[16,256,512]{2,1,0:T(8,128)S(1)} %convert_element_type.63, f32[256,256]{1,0:T(8,128)S(1)} %get-tuple-element.113, f32[256,256]{1,0:T(8,128)S(1)} %get-tuple-element.114), kind=kLoop, calls=%fused_computation.13.clone.1 | loop fusion | flops 8388608 | bytes 13107200 | tf_op jit(solution)/shard_map/convert.2
  55.3 0.9 copy-done
  56.3 10.8 %fusion.76 = f32[16,256,512]{2,1,0:T(8,128)} fusion(bf16[2,16,256,512]{3,2,1,0:T(8,128)(2,1)} %get-tuple-element.141, s32[]{:T(128)} %get-tuple-element.127, f32[512]{0:T(512)S(1)} %add_convert_fusion.3, bf16[16,256,256]{2,1,0:T(8,128)(2,1)} %get-tuple-element.115, bf16[16,256,256]{2,1,0:T(8,128)(2,1)S(1)} %get-tuple-element.116, ...), kind=kOutput, calls=%fused_computation.3.clone.1 | convolution fusion | flops 4311744512 | bytes 17828352 | tf_op jit(solution)/shard_map/while/body/eval_jaxpr/dot_general | solution.py:90
  67.1 7.0 %add_reduce_fusion.2 = (f32[256,256]{1,0:T(8,128)S(1)}, f32[256,256]{1,0:T(8,128)S(1)}) fusion(f32[16,256,512]{2,1,0:T(8,128)} %fusion.76, f32[16,256,512]{2,1,0:T(8,128)} %copy-done), kind=kLoop, calls=%fused_computation.10.clone.1 | loop fusion | flops 8257536 | bytes 17301504 | tf_op jit(solution)/shard_map/while/body/eval_jaxpr/reduce_sum | solution.py:96
  74.2 1.0 copy-done.3
  75.2 3.3 %convert_element_type.63 = f32[16,256,512]{2,1,0:T(8,128)S(1)} convert(bf16[16,256,512]{2,1,0:T(8,128)(2,1)} %get-tuple-element.137) | non-fusion elementwise | flops 2097152 | bytes 12582912 | tf_op jit(solution)/shard_map/while/body/eval_jaxpr/convert_element_type | solution.py:78
  78.6 2.9 %subtract_convert_fusion.2 = (bf16[16,256,256]{2,1,0:T(8,128)(2,1)S(1)}, bf16[16,256,256]{2,1,0:T(8,128)(2,1)}) fusion(f32[16,256,512]{2,1,0:T(8,128)S(1)} %convert_element_type.63, f32[256,256]{1,0:T(8,128)S(1)} %get-tuple-element.113, f32[256,256]{1,0:T(8,128)S(1)} %get-tuple-element.114), kind=kLoop, calls=%fused_computation.13.clone.1 | loop fusion | flops 8388608 | bytes 13107200 | tf_op jit(solution)/shard_map/convert.2
  81.5 0.9 copy-done
  82.4 10.8 %fusion.76 = f32[16,256,512]{2,1,0:T(8,128)} fusion(bf16[2,16,256,512]{3,2,1,0:T(8,128)(2,1)} %get-tuple-element.141, s32[]{:T(128)} %get-tuple-element.127, f32[512]{0:T(512)S(1)} %add_convert_fusion.3, bf16[16,256,256]{2,1,0:T(8,128)(2,1)} %get-tuple-element.115, bf16[16,256,256]{2,1,0:T(8,128)(2,1)S(1)} %get-tuple-element.116, ...), kind=kOutput, calls=%fused_computation.3.clone.1 | convolution fusion | flops 4311744512 | bytes 17828352 | tf_op jit(solution)/shard_map/while/body/eval_jaxpr/dot_general | solution.py:90
  93.2 7.0 %add_reduce_fusion.2 = (f32[256,256]{1,0:T(8,128)S(1)}, f32[256,256]{1,0:T(8,128)S(1)}) fusion(f32[16,256,512]{2,1,0:T(8,128)} %fusion.76, f32[16,256,512]{2,1,0:T(8,128)} %copy-done), kind=kLoop, calls=%fused_computation.10.clone.1 | loop fusion | flops 8257536 | bytes 17301504 | tf_op jit(solution)/shard_map/while/body/eval_jaxpr/reduce_sum | solution.py:96
  100.3 1.0 copy-done.3
  101.3 6.8 %reduce-scatter.2.cloned.1.call-done = f32[2,128,512]{2,1,0:T(8,128)} async-done(((f32[2,256,512]{2,1,0:T(8,128)}), f32[2,128,512]{2,1,0:T(8,128)}) %reduce-scatter.2.cloned.1.call-update) | async-done | bytes 524304 | tf_op jit(solution)/shard_map/reduce_scatter | solution.py:113
  108.1 1.1 convert_element_type.43
  114.1 5.8 %all-to-all-start.1 = ((bf16[8,2,16,512]{3,2,1,0:T(8,128)(2,1)}), bf16[8,2,16,512]{3,2,1,0:T(8,128)(2,1)S(1)}, u32[]{:S(2)}, u32[]{:S(2)}) async-start(bf16[8,2,16,512]{3,2,1,0:T(8,128)(2,1)} %fusion.54), calls=%async_computation.2 | async-start | bytes 524288 | tf_op jit(solution)/shard_map/all_to_all | solution.py:11
  121.2 8.1 %all-to-all-done.1 = bf16[8,2,16,512]{3,2,1,0:T(8,128)(2,1)S(1)} async-done(((bf16[8,2,16,512]{3,2,1,0:T(8,128)(2,1)}), bf16[8,2,16,512]{3,2,1,0:T(8,128)(2,1)S(1)}, u32[]{:S(2)}, u32[]{:S(2)}) %all-to-all-start.1) | async-done | bytes 262176 | tf_op jit(solution)/shard_map/all_to_all | solution.py:11
  130.7 19.7 %all-reduce = f32[16,64]{1,0:T(8,128)S(1)} all-reduce(f32[16,64]{1,0:T(8,128)S(1)} %pad_maximum_fusion.2), channel_id=3, replica_groups=mesh['cuts'=2,'frame'=8,'coil'=2] {'frame'}, use_global_device_ids=true, to_apply=%region_5.6.clone | all-reduce | flops 1024 | bytes 8192
  150.4 3.0 %psum.7 = f32[2,64]{1,0:T(2,128)} all-reduce(f32[2,64]{1,0:T(2,128)S(1)} %constant_dynamic-slice_fusion.1), channel_id=1, replica_groups=mesh['cuts'=2,'frame'=8,'coil'=2] {'coil'}, use_global_device_ids=true, to_apply=%region_6.7 | all-reduce | flops 128 | bytes 1024 | tf_op jit(solution)/shard_map/psum | solution.py:121
  154.2 1.1 pad_maximum_fusion
  (49 shorter events, 8.1 us)
Async XLA Ops:
  7.2 41.7 %copy-start.4 = (s32[2,256]{1,0:T(2,128)S(1)}, s32[2,256]{1,0:T(2,128)}, u32[]{:S(2)}) copy-start(s32[2,256]{1,0:T(2,128)} %param.10) | copy-start | bytes 6148
  35.1 11.6 %all-to-all-start = ((bf16[16,16,512]{2,1,0:T(8,128)(2,1)}), bf16[16,16,512]{2,1,0:T(8,128)(2,1)S(1)}, u32[]{:S(2)}, u32[]{:S(2)}) async-start(bf16[16,16,512]{2,1,0:T(8,128)(2,1)} %copy.9), calls=%async_computation | async-start | bytes 524288 | tf_op jit(solution)/shard_map/all_to_all | solution.py:105
  38.5 69.6 %reduce-scatter.2.cloned.1.call-start = ((), (), s32[]{:S(2)}) async-start(), calls=%async_computation.3 | async-start | bytes 1572864 | tf_op jit(solution)/shard_map/reduce_scatter | solution.py:113
  48.9 71.1 %copy-start.5 = (u32[32]{0:T(128)S(1)}, u32[32]{0:T(128)}, u32[]{:S(2)}) copy-start(u32[32]{0:T(128)} %constant.43) | copy-start | bytes 388
  48.9 80.4 %copy-start.1 = (bf16[16,32,512]{2,1,0:T(8,128)(2,1)S(1)}, bf16[16,32,512]{2,1,0:T(8,128)(2,1)}, u32[]{:S(2)}) copy-start(bf16[16,32,512]{2,1,0:T(8,128)(2,1)} %param.7) | copy-start | bytes 1572868
  52.4 3.8 %copy-start = (f32[16,256,512]{2,1,0:T(8,128)}, f32[16,256,512]{2,1,0:T(8,128)S(1)}, u32[]{:S(2)}) copy-start(f32[16,256,512]{2,1,0:T(8,128)S(1)} %convert_element_type.63) | copy-start | bytes 25165828 | tf_op jit(solution)/shard_map/while
  67.1 7.0 %copy-start.2 = (f32[2,256,512]{2,1,0:T(8,128)S(1)}, f32[2,256,512]{2,1,0:T(8,128)}, u32[]{:S(2)}) copy-start(f32[2,256,512]{2,1,0:T(8,128)} %get-tuple-element.128) | copy-start | bytes 3145732 | tf_op jit(solution)/shard_map/while
  74.2 1.0 copy-start.3
  78.6 3.8 %copy-start = (f32[16,256,512]{2,1,0:T(8,128)}, f32[16,256,512]{2,1,0:T(8,128)S(1)}, u32[]{:S(2)}) copy-start(f32[16,256,512]{2,1,0:T(8,128)S(1)} %convert_element_type.63) | copy-start | bytes 25165828 | tf_op jit(solution)/shard_map/while
  93.2 7.0 %copy-start.2 = (f32[2,256,512]{2,1,0:T(8,128)S(1)}, f32[2,256,512]{2,1,0:T(8,128)}, u32[]{:S(2)}) copy-start(f32[2,256,512]{2,1,0:T(8,128)} %get-tuple-element.128) | copy-start | bytes 3145732 | tf_op jit(solution)/shard_map/while
  100.3 1.0 copy-start.3
  114.1 15.2 %all-to-all-start.1 = ((bf16[8,2,16,512]{3,2,1,0:T(8,128)(2,1)}), bf16[8,2,16,512]{3,2,1,0:T(8,128)(2,1)S(1)}, u32[]{:S(2)}, u32[]{:S(2)}) async-start(bf16[8,2,16,512]{3,2,1,0:T(8,128)(2,1)} %fusion.54), calls=%async_computation.2 | async-start | bytes 524288 | tf_op jit(solution)/shard_map/all_to_all | solution.py:11
Sparse Core Ops, SparseCore 0:
  101.5 6.6 reduce-scatter.1
